TPU v7x, 512 devices: a whole 4x8x8 slice. The times are simulated.
512 devices in a mesh: occi: 16 (over y_lo, z), occj: 32 (over y_hi, x, core).
Axes of the slice: x: 4, y: 8 (y_hi: 4, y_lo: 2; y = y_hi * 2 + y_lo), z: 8, core: 2. Of those that a mesh axis runs over, the one named last changes fastest.
Arguments:
- amplitudes: float32 [32, 32, 512, 512], P('occi', 'occj'), may hold values from -6 to 6
- vectors: bfloat16 [3, 512, 512], P(None, 'occj'), may hold values from -0.25 to 0.25
- occupied_fock_block: bfloat16 [32, 32], replicated, may hold values from -1 to 1
- occ_energy: float32 [32], replicated, may hold values from -3 to -0.3
- vir_energy: float32 [512], replicated, may hold values from 0.2 to 4
Outputs:
- updated: float32 [32, 32, 512, 512], P('occi', 'occj')
All inputs are finite; a program needn't handle non-finite values.
Results may differ from a plain program's by a relative error of at most 0.0028.
Values may be sent and summed in bfloat16 or wider, within the bound.
A program may use at most 64 MiB of HBM per device.

v0:
```python
import jax
import jax.numpy as jnp
from jax import lax
from jax.sharding import PartitionSpec as P

ITERS = 2


def ladder_term(reduced_precision_copy, gathered):
    running = jnp.zeros(reduced_precision_copy.shape, jnp.float32)
    for vector_id in range(gathered.shape[0]):
        single = gathered[vector_id]
        inner = jnp.einsum(
            "pjcd,bd->pjcb", reduced_precision_copy, single, preferred_element_type=jnp.float32
        ).astype(jnp.bfloat16)
        running = running + jnp.einsum(
            "ac,pjcb->pjab", single, inner, preferred_element_type=jnp.float32
        )
    return running.astype(jnp.bfloat16)


def occupied_fock_blend(slab_partitioned, occupied_fock_block):
    flattened_row_list = slab_partitioned.reshape(slab_partitioned.shape[0], -1)
    contracted_result = lax.dot_general(
        occupied_fock_block,
        flattened_row_list,
        (((0,), (0,)), ((), ())),
        preferred_element_type=jnp.float32,
    )
    return -contracted_result.reshape(slab_partitioned.shape)


def to_mirror(half_slab):
    moved = lax.all_to_all(
        lax.all_to_all(half_slab, "occj", split_axis=0, concat_axis=1, tiled=True),
        "occi",
        split_axis=1,
        concat_axis=2,
        tiled=True,
    )
    return jnp.transpose(moved, (1, 0, 3, 2))


def local(amplitudes, vectors, occupied_fock_block, occ_energy, vir_energy):
    gathered = lax.all_gather(vectors, "occj", axis=1, tiled=True)
    rows_first = amplitudes.shape[0]
    rows_second = amplitudes.shape[1]
    occ_first = lax.dynamic_slice_in_dim(
        occ_energy, lax.axis_index("occi") * rows_first, rows_first
    )
    occ_second = lax.dynamic_slice_in_dim(
        occ_energy, lax.axis_index("occj") * rows_second, rows_second
    )
    denominator = (
        occ_first[:, None, None, None]
        + occ_second[None, :, None, None]
        - vir_energy[None, None, :, None]
        - vir_energy[None, None, None, :]
    )
    current = amplitudes
    for iteration in range(ITERS):
        reduced_precision_copy = current.astype(jnp.bfloat16)
        slab_partitioned = lax.all_to_all(
            reduced_precision_copy, "occi", split_axis=2, concat_axis=0, tiled=True
        )
        ladder = ladder_term(reduced_precision_copy, gathered)
        blended_amplitude = occupied_fock_blend(slab_partitioned, occupied_fock_block)
        mixed_home = lax.all_to_all(
            blended_amplitude, "occi", split_axis=0, concat_axis=2, tiled=True
        )
        ladder_wide = lax.optimization_barrier(ladder).astype(jnp.float32)
        halfway = (ladder_wide + mixed_home).astype(jnp.bfloat16)
        half_slab = lax.all_to_all(halfway, "occi", split_axis=2, concat_axis=0, tiled=True)
        mirrored = to_mirror(half_slab)
        residual = halfway.astype(jnp.float32) + mirrored.astype(jnp.float32)
        current = current + residual / denominator
    return current


def solution(mesh):
    return jax.shard_map(
        local,
        mesh=mesh,
        in_specs=(P("occi", "occj", None, None), P(None, "occj", None), P(), P(), P()),
        out_specs=P("occi", "occj", None, None),
        check_vma=False,
    )
```

profile of v0, /device:TPU:1, one launch (start us, length us, event | category | flops | bytes accessed | tf_op | source)
XLA Modules:
  0.0 432.1 jit_solution(6795098370082269042)
XLA Ops:
  8.3 2.0 copy.111
  10.3 12.0 %all-to-all-start = ((bf16[2,1,512,512]{3,0,1,2:T(2,128)(2,1)}), bf16[2,1,512,512]{3,0,1,2:T(2,128)(2,1)S(1)}, u32[]{:S(2)}, u32[]{:S(2)}) async-start(bf16[2,1,512,512]{3,0,1,2:T(2,128)(2,1)} %copy.111), calls=%async_computation | async-start | bytes 2097152 | tf_op jit(solution)/shard_map/all_to_all | solution.py:63
  23.0 24.7 %all-to-all-done = bf16[2,1,512,512]{3,0,1,2:T(2,128)(2,1)S(1)} async-done(((bf16[2,1,512,512]{3,0,1,2:T(2,128)(2,1)}), bf16[2,1,512,512]{3,0,1,2:T(2,128)(2,1)S(1)}, u32[]{:S(2)}, u32[]{:S(2)}) %all-to-all-start) | async-done | bytes 1048608 | tf_op jit(solution)/shard_map/all_to_all | solution.py:63
  48.9 2.5 copy.116
  51.5 7.2 %all-to-all-start.1 = ((f32[32,1,32,512]{3,2,1,0:T(8,128)}), f32[32,1,32,512]{3,2,1,0:T(8,128)S(1)}, u32[]{:S(2)}, u32[]{:S(2)}) async-start(f32[32,1,32,512]{3,2,1,0:T(8,128)} %copy.116), calls=%async_computation.1 | async-start | bytes 4194304 | tf_op jit(solution)/shard_map/all_to_all | solution.py:68
  58.7 28.6 %all-gather.2.cloned.1.call-done = bf16[3,512,512]{2,1,0:T(8,128)(2,1)} async-done(((bf16[3,16,512]{2,1,0:T(8,128)(2,1)}), bf16[3,512,512]{2,1,0:T(8,128)(2,1)}) %all-gather.2.cloned.1.call-update) | async-done | bytes 1572880 | tf_op jit(solution)/shard_map/all_gather | solution.py:45
  87.3 3.8 fusion.2
  91.2 3.8 fusion.3
  95.0 4.8 %fusion.6 = bf16[2,1,512,512]{2,3,0,1:T(8,128)(2,1)} fusion(f32[2,512,512]{2,1,0:T(8,128)} %fusion.2, f32[2,512,512]{2,1,0:T(8,128)} %fusion.3, bf16[2,1,512,512]{3,2,0,1:T(8,128)(2,1)S(1)} %bitcast_convert_fusion, bf16[3,512,512]{2,1,0:T(8,128)(2,1)} %all-gather.2.cloned.1.call-done), kind=kOutput, calls=%fused_computation.25 | convolution fusion | flops 1075838976 | bytes 7340032 | tf_op jit(solution)/shard_map/ac,pjcb->pjab/dot_general | solution.py:16
  99.8 10.6 %all-to-all-done.1 = f32[32,1,32,512]{3,2,1,0:T(8,128)S(1)} async-done(((f32[32,1,32,512]{3,2,1,0:T(8,128)}), f32[32,1,32,512]{3,2,1,0:T(8,128)S(1)}, u32[]{:S(2)}, u32[]{:S(2)}) %all-to-all-start.1) | async-done | bytes 2097184 | tf_op jit(solution)/shard_map/all_to_all | solution.py:68
  116.5 31.0 %all_to_all.144 = bf16[2,1,512,512]{3,0,1,2:T(2,128)(2,1)S(1)} all-to-all(bf16[2,1,512,512]{3,0,1,2:T(2,128)(2,1)S(1)} %copy.119), channel_id=1, replica_groups=mesh['occi'=16,'occj'=32] {'occi'}, dimensions={2} | all-to-all | bytes 2097152 | tf_op jit(solution)/shard_map/all_to_all | solution.py:73
  147.7 34.1 %all_to_all.145 = bf16[32,1,32,512]{3,2,1,0:T(8,128)(2,1)} all-to-all(bf16[32,1,32,512]{3,2,1,0:T(8,128)(2,1)S(1)} %bitcast.154), channel_id=1, replica_groups=mesh['occi'=16,'occj'=32] {'occj'}, dimensions={0} | all-to-all | bytes 2097152 | tf_op jit(solution)/shard_map/all_to_all | solution.py:35
  181.8 10.6 %all-to-all-start.4 = ((bf16[1,32,32,512]{3,2,0,1:T(8,128)(2,1)}), bf16[1,32,32,512]{3,2,0,1:T(8,128)(2,1)}, u32[]{:S(2)}, u32[]{:S(2)}) async-start(bf16[1,32,32,512]{3,2,0,1:T(8,128)(2,1)} %bitcast.151), calls=%async_computation.4 | async-start | bytes 2097152 | tf_op jit(solution)/shard_map/all_to_all | solution.py:34
  195.6 22.2 %all-to-all-done.4 = bf16[1,32,32,512]{3,2,0,1:T(8,128)(2,1)} async-done(((bf16[1,32,32,512]{3,2,0,1:T(8,128)(2,1)}), bf16[1,32,32,512]{3,2,0,1:T(8,128)(2,1)}, u32[]{:S(2)}, u32[]{:S(2)}) %all-to-all-start.4) | async-done | bytes 1048608 | tf_op jit(solution)/shard_map/all_to_all | solution.py:34
  223.7 31.4 %all_to_all.146 = bf16[2,1,512,512]{3,0,1,2:T(2,128)(2,1)S(1)} all-to-all(bf16[2,1,512,512]{3,0,1,2:T(2,128)(2,1)S(1)} %copy.133), channel_id=1, replica_groups=mesh['occi'=16,'occj'=32] {'occi'}, dimensions={2} | all-to-all | bytes 2097152 | tf_op jit(solution)/shard_map/all_to_all | solution.py:63
  256.4 2.6 copy.161
  259.0 7.6 %all-to-all-start.6 = ((f32[32,1,32,512]{3,2,1,0:T(8,128)}), f32[32,1,32,512]{3,2,1,0:T(8,128)S(1)}, u32[]{:S(2)}, u32[]{:S(2)}) async-start(f32[32,1,32,512]{3,2,1,0:T(8,128)} %bitcast.144), calls=%async_computation.6 | async-start | bytes 4194304 | tf_op jit(solution)/shard_map/all_to_all | solution.py:68
  266.6 3.9 fusion.4
  270.4 3.9 fusion.5
  274.4 4.9 %fusion.7 = bf16[2,1,512,512]{2,3,0,1:T(8,128)(2,1)} fusion(f32[2,512,512]{2,1,0:T(8,128)} %fusion.4, f32[2,512,512]{2,1,0:T(8,128)} %fusion.5, bf16[2,1,512,512]{2,3,0,1:T(8,128)(2,1)S(1)} %get-tuple-element.5, bf16[3,512,512]{2,1,0:T(8,128)(2,1)} %all-gather.2.cloned.1.call-done), kind=kOutput, calls=%fused_computation.26 | convolution fusion | flops 1075838976 | bytes 7340032 | tf_op jit(solution)/shard_map/ac,pjcb->pjab/dot_general | solution.py:16
  279.3 38.6 %all-to-all-done.6 = f32[32,1,32,512]{3,2,1,0:T(8,128)S(1)} async-done(((f32[32,1,32,512]{3,2,1,0:T(8,128)}), f32[32,1,32,512]{3,2,1,0:T(8,128)S(1)}, u32[]{:S(2)}, u32[]{:S(2)}) %all-to-all-start.6) | async-done | bytes 2097184 | tf_op jit(solution)/shard_map/all_to_all | solution.py:68
  323.9 31.2 %all_to_all.147 = bf16[2,1,512,512]{3,0,1,2:T(2,128)(2,1)S(1)} all-to-all(bf16[2,1,512,512]{3,0,1,2:T(2,128)(2,1)S(1)} %copy.139), channel_id=1, replica_groups=mesh['occi'=16,'occj'=32] {'occi'}, dimensions={2} | all-to-all | bytes 2097152 | tf_op jit(solution)/shard_map/all_to_all | solution.py:73
  355.4 30.8 %all_to_all.148 = bf16[32,1,32,512]{3,2,1,0:T(8,128)(2,1)S(1)} all-to-all(bf16[32,1,32,512]{3,2,1,0:T(8,128)(2,1)S(1)} %bitcast.158), channel_id=1, replica_groups=mesh['occi'=16,'occj'=32] {'occj'}, dimensions={0} | all-to-all | bytes 2097152 | tf_op jit(solution)/shard_map/all_to_all | solution.py:35
  386.2 34.8 %all_to_all.149 = bf16[1,32,32,512]{3,2,0,1:T(8,128)(2,1)S(1)} all-to-all(bf16[1,32,32,512]{3,2,0,1:T(8,128)(2,1)S(1)} %bitcast.159), channel_id=1, replica_groups=mesh['occi'=16,'occj'=32] {'occi'}, dimensions={1} | all-to-all | bytes 2097152 | tf_op jit(solution)/shard_map/all_to_all | solution.py:34
  (48 shorter events, 30.8 us)
Async XLA Ops:
  6.5 41.5 %copy-start = (bf16[32,32]{1,0:T(8,128)(2,1)S(1)}, bf16[32,32]{1,0:T(8,128)(2,1)}, u32[]{:S(2)}) copy-start(bf16[32,32]{1,0:T(8,128)(2,1)} %param.7) | copy-start | bytes 6148
  10.3 37.4 %all-to-all-start = ((bf16[2,1,512,512]{3,0,1,2:T(2,128)(2,1)}), bf16[2,1,512,512]{3,0,1,2:T(2,128)(2,1)S(1)}, u32[]{:S(2)}, u32[]{:S(2)}) async-start(bf16[2,1,512,512]{3,0,1,2:T(2,128)(2,1)} %copy.111), calls=%async_computation | async-start | bytes 2097152 | tf_op jit(solution)/shard_map/all_to_all | solution.py:63
  22.3 65.0 %all-gather.2.cloned.1.call-start = ((), (), s32[]{:S(2)}) async-start(), calls=%async_computation.10 | async-start | bytes 1622016 | tf_op jit(solution)/shard_map/all_gather | solution.py:45
  51.5 58.9 %all-to-all-start.1 = ((f32[32,1,32,512]{3,2,1,0:T(8,128)}), f32[32,1,32,512]{3,2,1,0:T(8,128)S(1)}, u32[]{:S(2)}, u32[]{:S(2)}) async-start(f32[32,1,32,512]{3,2,1,0:T(8,128)} %copy.116), calls=%async_computation.1 | async-start | bytes 4194304 | tf_op jit(solution)/shard_map/all_to_all | solution.py:68
  147.7 44.7 %copy-start.2 = (f32[2,1,512,512]{3,2,1,0:T(8,128)S(1)}, f32[2,1,512,512]{3,2,1,0:T(8,128)}, u32[]{:S(2)}) copy-start(f32[2,1,512,512]{3,2,1,0:T(8,128)} %param.5) | copy-start | bytes 6291460
  181.8 35.9 %all-to-all-start.4 = ((bf16[1,32,32,512]{3,2,0,1:T(8,128)(2,1)}), bf16[1,32,32,512]{3,2,0,1:T(8,128)(2,1)}, u32[]{:S(2)}, u32[]{:S(2)}) async-start(bf16[1,32,32,512]{3,2,0,1:T(8,128)(2,1)} %bitcast.151), calls=%async_computation.4 | async-start | bytes 2097152 | tf_op jit(solution)/shard_map/all_to_all | solution.py:34
  192.5 1.8 copy-start.6
  192.5 3.0 copy-start.5
  219.3 1.6 copy-start.3
  259.0 58.9 %all-to-all-start.6 = ((f32[32,1,32,512]{3,2,1,0:T(8,128)}), f32[32,1,32,512]{3,2,1,0:T(8,128)S(1)}, u32[]{:S(2)}, u32[]{:S(2)}) async-start(f32[32,1,32,512]{3,2,1,0:T(8,128)} %bitcast.144), calls=%async_computation.6 | async-start | bytes 4194304 | tf_op jit(solution)/shard_map/all_to_all | solution.py:68
  421.3 1.6 copy-start.4
  422.9 2.4 copy-start.1
Sparse Core Ops, SparseCore 0:
  26.3 60.9 all-gather.1
where the time goes:
time: 434 us; the launch traced here: 432 us
  blocking collectives  193 us (44%)
  waiting for transfers between devices  125 us (29%)
  starting transfers between devices  37.4 us (9%)
  matrix products  26.6 us (6%)
  local copies, waits for them, and re-layouts  26.1 us (6%)
  between operations  13.7 us (3%)
  other arithmetic  9.75 us (2%)
    all_to_all x2, blocking collectives, to_mirror(): lax.all_to_all(half_slab, 'occj', split_axis=0, concat_axis=1, tiled=True)  64.9 us
    all_to_all x2, blocking collectives, local(): lax.all_to_all(halfway, 'occi', split_axis=2, concat_axis=0, tiled=True)  62.2 us
    all_to_all x2, waiting for transfers between devices, local(): lax.all_to_all(blended_amplitude, 'occi', split_axis=0, concat_axis=2, ti...  49.2 us
    all_to_all x1, blocking collectives, to_mirror(): lax.all_to_all(lax.all_to_all(half_slab, 'occj', split_axis=0, concat_axi...  34.8 us
    all_to_all x1, blocking collectives, local(): lax.all_to_all(reduced_precision_copy, 'occi', split_axis=2, concat_axis=...  31.4 us
    all_gather x1, waiting for transfers between devices, local(): gathered = lax.all_gather(vectors, 'occj', axis=1, tiled=True)  28.6 us
    dot_general x6, matrix products, ladder_term(): jnp.einsum('ac,pjcb->pjab', single, inner, preferred_element_type=jnp.flo...  25.2 us
    all_to_all x1, waiting for transfers between devices, local(): lax.all_to_all(reduced_precision_copy, 'occi', split_axis=2, concat_axis=...  24.7 us
  transfers between devices with their start and end apart: 5, of which 5 were waited for; matrix products, arithmetic and copies ran while one was open for 7% of the time, Pallas kernels for 0%

commit v1 on v0

v1 whole, which is shorter than its diff:
```python
import functools

import jax
import jax.numpy as jnp
from jax import lax
from jax.experimental import pallas as pl
from jax.experimental.pallas import tpu as pltpu
from jax.sharding import PartitionSpec as P

MESH = pl.DeviceIdType.MESH
NI, NJ = 16, 32
B = 128
PAIRS = ((0, 1), (0, 2), (0, 3), (1, 2), (1, 3), (2, 3))
PLACES = PAIRS + ((0, 0), (2, 2)) + tuple((b, a) for a, b in PAIRS) + ((1, 1), (3, 3))


def kernel(
    amp_ref, vec_ref, fock_ref, occ_ref, vir_ref, out_ref,
    t0, tb, vg, kron, inner, blk, tsl, lblk, lsl, mix, hs, hm, us, uh, ms, hm2, ws, wh, lu,
    amp_sem, vs_sem, vr_sem, xs_sem, xr_sem, ts_sem, tr_sem, ls_sem, lr_sem,
    hs_sem, hr_sem, us_sem, ur_sem, ms_sem, mr_sem, ws_sem, wr_sem,
):
    p = lax.axis_index("occi")
    q = lax.axis_index("occj")
    ylo, z = p // 8, p % 8
    r, core = q // 2, q % 2
    yhi, x = r // 4, r % 4
    flip = (p + 8) % NI
    mirror = (p + 8 * (1 - z // 6)) % NI

    load = pltpu.make_async_copy(amp_ref, t0, amp_sem)
    load.start()

    barrier = pltpu.get_barrier_semaphore()

    def greet(dev):
        pl.semaphore_signal(barrier, inc=1, device_id=dev, device_id_type=MESH)

    def greet_column(t, c):
        greet(((p + t) % NI, q))
        return c

    def greet_row(t, c):
        greet((p, (q + t) % NJ))
        greet((flip, (q + t) % NJ))
        return c

    lax.fori_loop(1, NI, greet_column, 0)
    lax.fori_loop(1, NJ, greet_row, 0)

    rows = lax.broadcasted_iota(jnp.int32, (512, NJ), 0) // 16
    cols = lax.broadcasted_iota(jnp.int32, (512, NJ), 1)
    spread = (rows == cols).astype(jnp.float32).astype(jnp.bfloat16)
    wide = lax.dot_general(
        fock_ref[...], spread, (((0,), (1,)), ((), ())), preferred_element_type=jnp.float32
    ).astype(jnp.bfloat16)
    tall = jnp.dot(spread, wide, preferred_element_type=jnp.float32)
    same = (
        lax.broadcasted_iota(jnp.int32, (512, 512), 0) % 16
        == lax.broadcasted_iota(jnp.int32, (512, 512), 1) % 16
    )
    kron[...] = jnp.where(same, -tall, 0.0).astype(jnp.bfloat16)

    load.wait()
    for s in range(2):
        for place, (ka, kb) in enumerate(PLACES):
            part = t0[s, ka * B:(ka + 1) * B, kb * B:(kb + 1) * B].astype(jnp.bfloat16)
            blk[place, s] = part
            tb[s, ka * B:(ka + 1) * B, kb * B:(kb + 1) * B] = part

    pl.semaphore_wait(barrier, NI - 1 + 2 * (NJ - 1))

    vg[:, r, core] = vec_ref[...]
    sign = 2 * ylo - 1
    y = 2 * yhi + ylo

    def send_vec(ty, tx):
        ny = (y + sign * ty + 8) % 8
        nx = (x + tx) % 4
        pltpu.make_async_remote_copy(
            vec_ref, vg.at[:, r, core], vs_sem, vr_sem,
            device_id=((ny % 2) * 8 + z, ((ny // 2) * 4 + nx) * 2 + core), device_id_type=MESH,
        ).start()

    def send_vec_far(t, c):
        send_vec(1 + t // 4, t % 4)
        return c

    def send_vec_near(t, c):
        send_vec(0, t)
        return c

    lax.fori_loop(0, 12, send_vec_far, 0)
    lax.fori_loop(1, 4, send_vec_near, 0)

    def send_block(src, dst, send, recv, k):
        @pl.when(k != p)
        def _():
            pltpu.make_async_remote_copy(
                src, dst, send, recv, device_id=(k, q), device_id_type=MESH
            ).start()

        @pl.when(k == p)
        def _():
            pltpu.make_async_copy(src, dst, recv).start()

    def send_t(t, c):
        zi = t // 2
        dz = ((zi + 1) // 2) * (2 * (zi % 2) - 1)
        k = ((ylo + t % 2) % 2) * 8 + (z + dz + 8) % 8
        send_block(blk.at[k], tsl.at[pl.ds(2 * p, 2)], ts_sem, tr_sem, k)
        return c

    lax.fori_loop(0, NI, send_t, 0)

    most = vg.at[:, pl.ds(0, 15), 0]
    pltpu.make_async_copy(most, most, vr_sem).wait()
    other = 2 * r + 1 - core
    swap = pltpu.make_async_remote_copy(
        vg.at[:, :, core], vg.at[:, :, core], xs_sem, xr_sem,
        device_id=(p, other), device_id_type=MESH,
    )
    swap.start()
    swap.wait_send()
    pltpu.make_async_copy(vg.at[:, :, 0], vg.at[:, :, 0], xr_sem).wait()

    def ladder(source, store):
        def first(s, c):
            for h in range(2):
                piece = source[s, h * 256:(h + 1) * 256, :]
                for l in range(3):
                    inner[s, l, h * 256:(h + 1) * 256, :] = lax.dot_general(
                        piece, vg[l].reshape(512, 512), (((1,), (1,)), ((), ())),
                        preferred_element_type=jnp.float32,
                    ).astype(jnp.bfloat16)
            return c

        def second(s, c):
            for h in range(2):
                total = None
                for l in range(3):
                    term = jnp.dot(
                        vg[l, h * 8:(h + 1) * 8].reshape(256, 512), inner[s, l],
                        preferred_element_type=jnp.float32,
                    )
                    total = term if total is None else total + term
                store(s, h, total)
            return c

        lax.fori_loop(0, 2, first, 0)
        lax.fori_loop(0, 2, second, 0)

    def store_blocks(s, h, total):
        for place, (ka, kb) in enumerate(PLACES):
            if ka // 2 == h:
                lblk[place, s] = total[(ka % 2) * B:(ka % 2 + 1) * B, kb * B:(kb + 1) * B].astype(jnp.bfloat16)

    ladder(tb, store_blocks)

    def send_l(t, c):
        k = (p + 2 * NI - r - t) % NI
        send_block(lblk.at[k], lsl.at[pl.ds(2 * p, 2)], ls_sem, lr_sem.at[p], k)
        return c

    lax.fori_loop(0, NI, send_l, 0)

    def mixing(source):
        def group(g, c):
            lines = pl.ds(pl.multiple_of(g * 16, 16), 16)
            got = jnp.dot(
                kron[...], source[:, lines, :].reshape(512, B), preferred_element_type=jnp.float32
            )
            mix[:, lines, :] = got.reshape(NJ, 16, B)
            return c

        lax.fori_loop(0, B // 16, group, 0)

    pltpu.make_async_copy(tsl, tsl, tr_sem).wait()
    mixing(tsl)

    def send_mirror(src, dst, send, recv, i):
        alone = (mirror == p) & (i == q)

        @pl.when(jnp.logical_not(alone))
        def _():
            pltpu.make_async_remote_copy(
                src, dst, send, recv, device_id=(mirror, i), device_id_type=MESH
            ).start()

        @pl.when(alone)
        def _():
            pltpu.make_async_copy(src, dst, recv).start()

    def halves(t, c):
        k = (p + r + t) % NI
        pltpu.make_async_copy(lblk.at[0], lsl.at[pl.ds(2 * k, 2)], lr_sem.at[k]).wait()
        for s in range(2):
            i = 2 * k + s
            hs[i] = (mix[i] + lsl[i].astype(jnp.float32)).astype(jnp.bfloat16)
            send_mirror(hs.at[i], hm.at[q], hs_sem, hr_sem.at[q], i)
        return c

    lax.fori_loop(0, NI, halves, 0)

    va = jnp.zeros((1, B), jnp.float32)
    vb = jnp.zeros((1, B), jnp.float32)
    for place, (ka, kb) in enumerate(PLACES):
        here = p == place
        va = jnp.where(here, vir_ref[ka:ka + 1, :], va)
        vb = jnp.where(here, vir_ref[kb:kb + 1, :], vb)
    va_block = jnp.transpose(jnp.broadcast_to(va, (B, B)))
    occ_j = occ_ref[q]

    def updates(t, c):
        k = (r + 2 * NI - mirror - t) % NI
        for s in range(2):
            i = 2 * k + s
            pltpu.make_async_copy(hs.at[0], hm.at[i], hr_sem.at[i]).wait()
            residual = hs[i].astype(jnp.float32) + jnp.transpose(hm[i].astype(jnp.float32))
            denominator = ((occ_ref[i] + occ_j) - va_block) - vb
            us[i] = (residual / denominator).astype(jnp.bfloat16)
        send_block(us.at[pl.ds(2 * k, 2)], uh.at[p], us_sem, ur_sem, k)
        return c

    lax.fori_loop(0, NI, updates, 0)

    mixing(us)

    def send_mix(t, c):
        k = (r + t) % NI
        for s in range(2):
            i = 2 * k + s
            ms[i] = mix[i].astype(jnp.bfloat16)
            send_mirror(ms.at[i], hm2.at[q], ms_sem, mr_sem.at[q], i)
        return c

    lax.fori_loop(0, NI, send_mix, 0)

    def sums(t, c):
        k = (r + NI - t) % NI
        for s in range(2):
            i = 2 * k + s
            pltpu.make_async_copy(ms.at[0], hm2.at[i], mr_sem.at[i]).wait()
            ws[i] = (mix[i] + jnp.transpose(hm2[i].astype(jnp.float32))).astype(jnp.bfloat16)
        send_block(ws.at[pl.ds(2 * k, 2)], wh.at[p], ws_sem, wr_sem, k)
        return c

    lax.fori_loop(0, NI, sums, 0)

    pltpu.make_async_copy(uh, uh, ur_sem).wait()
    for s in range(2):
        for place, (ka, kb) in enumerate(PLACES):
            tb[s, ka * B:(ka + 1) * B, kb * B:(kb + 1) * B] = uh[place, s]

    def store_plain(s, h, total):
        lu[s, h * 256:(h + 1) * 256, :] = total

    ladder(tb, store_plain)

    pltpu.make_async_copy(wh, wh, wr_sem).wait()
    for ka in range(4):
        va_block = jnp.transpose(jnp.broadcast_to(vir_ref[ka:ka + 1, :], (B, B)))
        for kb in range(4):
            place = PLACES.index((ka, kb))
            at = (slice(ka * B, (ka + 1) * B), slice(kb * B, (kb + 1) * B))
            for s in range(2):
                denominator = ((occ_ref[2 * p + s] + occ_j) - va_block) - vir_ref[kb:kb + 1, :]
                residual = 2.0 * lu[(s,) + at] + wh[place, s].astype(jnp.float32)
                out_ref[(s,) + at] = (
                    t0[(s,) + at] + 2.0 * uh[place, s].astype(jnp.float32) + residual / denominator
                )

    pltpu.make_async_copy(most, most, vs_sem).wait()
    rest = pl.ds(0, NI - 1)
    pltpu.make_async_copy(blk.at[rest], blk.at[rest], ts_sem).wait()
    pltpu.make_async_copy(lblk.at[rest], lblk.at[rest], ls_sem).wait()
    pltpu.make_async_copy(uh.at[rest], uh.at[rest], us_sem).wait()
    pltpu.make_async_copy(wh.at[rest], wh.at[rest], ws_sem).wait()
    alone = mirror == p

    @pl.when(alone)
    def _():
        left = pl.ds(0, NJ - 1)
        pltpu.make_async_copy(hs.at[left], hs.at[left], hs_sem).wait()
        pltpu.make_async_copy(ms.at[left], ms.at[left], ms_sem).wait()

    @pl.when(jnp.logical_not(alone))
    def _():
        pltpu.make_async_copy(hs, hs, hs_sem).wait()
        pltpu.make_async_copy(ms, ms, ms_sem).wait()


def local(amplitudes, vectors, occupied_fock_block, occ_energy, vir_energy):
    bf, f32 = jnp.bfloat16, jnp.float32
    dma = pltpu.SemaphoreType.DMA
    vmem = pl.BlockSpec(memory_space=pltpu.VMEM)
    out = pl.pallas_call(
        kernel,
        out_shape=jax.ShapeDtypeStruct((2, 512, 512), f32),
        in_specs=[
            pl.BlockSpec(memory_space=pl.ANY), vmem, vmem,
            pl.BlockSpec(memory_space=pltpu.SMEM), vmem,
        ],
        out_specs=vmem,
        scratch_shapes=[
            pltpu.VMEM((2, 512, 512), f32),
            pltpu.VMEM((2, 512, 512), bf),
            pltpu.VMEM((3, 16, 2, 16, 512), bf),
            pltpu.VMEM((512, 512), bf),
            pltpu.VMEM((2, 3, 512, 512), bf),
            pltpu.VMEM((NI, 2, B, B), bf),
            pltpu.VMEM((NJ, B, B), bf),
            pltpu.VMEM((NI, 2, B, B), bf),
            pltpu.VMEM((NJ, B, B), bf),
            pltpu.VMEM((NJ, B, B), f32),
            pltpu.VMEM((NJ, B, B), bf),
            pltpu.VMEM((NJ, B, B), bf),
            pltpu.VMEM((NJ, B, B), bf),
            pltpu.VMEM((NI, 2, B, B), bf),
            pltpu.VMEM((NJ, B, B), bf),
            pltpu.VMEM((NJ, B, B), bf),
            pltpu.VMEM((NJ, B, B), bf),
            pltpu.VMEM((NI, 2, B, B), bf),
            pltpu.VMEM((2, 512, 512), f32),
            dma, dma, dma, dma, dma, dma, dma,
            dma, dma((NI,)), dma, dma((NJ,)),
            dma, dma, dma, dma((NJ,)), dma, dma,
        ],
        compiler_params=pltpu.CompilerParams(
            collective_id=0, has_side_effects=True, vmem_limit_bytes=60 * 1024 * 1024
        ),
        name="doubles",
    )(
        amplitudes.reshape(2, 512, 512), vectors, occupied_fock_block, occ_energy,
        vir_energy.reshape(4, B),
    )
    return out.reshape(2, 1, 512, 512)


def solution(mesh):
    return jax.shard_map(
        local,
        mesh=mesh,
        in_specs=(P("occi", "occj", None, None), P(None, "occj", None), P(), P(), P()),
        out_specs=P("occi", "occj", None, None),
        check_vma=False,
    )
```

time: 434 us -> 160 us (0.37)
  the two profiles are of different devices: /device:TPU:1 before, /device:TPU:29 now
where the time goes in v1:
time: 160 us
  Pallas kernels  157 us (98%)
  local copies, waits for them, and re-layouts  3.08 us (2%)
    pallas_call x1, Pallas kernels, local(): pl.pallas_call(kernel, out_shape=jax.ShapeDtypeStruct((2, 512, 512), f32)...  157 us

profile of v1, /device:TPU:29, one launch (start us, length us, event | category | flops | bytes accessed | tf_op | source)
XLA Modules:
  0.0 159.7 jit_solution(10244067749933486631)
XLA Ops:
  0.0 156.6 %doubles.1 = f32[2,512,512]{2,1,0:T(8,128)} custom-call(f32[2,512,512]{2,1,0:T(8,128)} %bitcast.6, bf16[3,16,512]{2,1,0:T(8,128)(2,1)} %vec_ref.1, bf16[32,32]{1,0:T(8,128)(2,1)} %fock_ref.1, f32[32]{0:T(128)} %occ_ref.1, f32[4,128]{1,0:T(4,128)} %bitcast.7), custom_call_target="tpu_custom_call" | custom-call | tf_op jit(solution)/shard_map/doubles/pallas_call | solution.py:297
  156.6 3.1 %copy.8 = f32[2,1,512,512]{3,2,1,0:T(8,128)} copy(f32[2,1,512,512]{3,2,1,0:T(8,128)} %bitcast.5) | data formatting | bytes 4194304

commit v2 on v1

--- a/solution.py
+++ b/solution.py
@@ -16,8 +16,8 @@
 
 def kernel(
     amp_ref, vec_ref, fock_ref, occ_ref, vir_ref, out_ref,
-    t0, tb, vg, kron, inner, blk, tsl, lblk, lsl, mix, hs, hm, us, uh, ms, hm2, ws, wh, lu,
-    amp_sem, vs_sem, vr_sem, xs_sem, xr_sem, ts_sem, tr_sem, ls_sem, lr_sem,
+    t0, tb, tfl, vg, kron, inner, blk, tsl, lblk, lsl, mix, hs, hst, hm, us, uh, ms, hm2, ws, wh, lu,
+    amp_sem, vs_sem, vr_sem, xs_sem, xr_sem, ts_sem, tr_sem, tfs_sem, tfr_sem, tgs_sem, tgr_sem, ls_sem, lr_sem,
     hs_sem, hr_sem, us_sem, ur_sem, ms_sem, mr_sem, ws_sem, wr_sem,
 ):
     p = lax.axis_index("occi")
@@ -25,7 +25,10 @@
     ylo, z = p // 8, p % 8
     r, core = q // 2, q % 2
     yhi, x = r // 4, r % 4
+    y = 2 * yhi + ylo
+    other = 2 * r + 1 - core
     flip = (p + 8) % NI
+    ours, theirs = 8 * ylo, 8 * (1 - ylo)
     mirror = (p + 8 * (1 - z // 6)) % NI
 
     load = pltpu.make_async_copy(amp_ref, t0, amp_sem)
@@ -40,13 +43,31 @@
         greet(((p + t) % NI, q))
         return c
 
-    def greet_row(t, c):
-        greet((p, (q + t) % NJ))
-        greet((flip, (q + t) % NJ))
-        return c
-
+    def at_y(ny, nx):
+        return ((ny % 2) * 8 + z, ((ny // 2) * 4 + nx) * 2 + core)
+
+    def greet_mirror(i, c):
+        @pl.when(jnp.logical_not((mirror == p) & (i == q)))
+        def _():
+            greet((mirror, i))
+
+        return c
+
+    def greet_vec_near(t, c):
+        greet(at_y(y, (x + t) % 4))
+        return c
+
+    def greet_vec_far(t, c):
+        d = 1 + t // 4
+        up = (d + y) % 2
+        greet(at_y((y - d * up + d * (1 - up) + 8) % 8, (x + t) % 4))
+        return c
+
+    greet((p, other))
     lax.fori_loop(1, NI, greet_column, 0)
-    lax.fori_loop(1, NJ, greet_row, 0)
+    lax.fori_loop(1, 4, greet_vec_near, 0)
+    lax.fori_loop(0, 12, greet_vec_far, 0)
+    lax.fori_loop(0, NJ, greet_mirror, 0)
 
     rows = lax.broadcasted_iota(jnp.int32, (512, NJ), 0) // 16
     cols = lax.broadcasted_iota(jnp.int32, (512, NJ), 1)
@@ -68,18 +89,15 @@
             blk[place, s] = part
             tb[s, ka * B:(ka + 1) * B, kb * B:(kb + 1) * B] = part
 
-    pl.semaphore_wait(barrier, NI - 1 + 2 * (NJ - 1))
+    pl.semaphore_wait(barrier, 1 + NI - 1 + 15 + NJ - z // 6)
 
     vg[:, r, core] = vec_ref[...]
     sign = 2 * ylo - 1
-    y = 2 * yhi + ylo
 
     def send_vec(ty, tx):
-        ny = (y + sign * ty + 8) % 8
-        nx = (x + tx) % 4
         pltpu.make_async_remote_copy(
             vec_ref, vg.at[:, r, core], vs_sem, vr_sem,
-            device_id=((ny % 2) * 8 + z, ((ny // 2) * 4 + nx) * 2 + core), device_id_type=MESH,
+            device_id=at_y((y + sign * ty + 8) % 8, (x + tx) % 4), device_id_type=MESH,
         ).start()
 
     def send_vec_far(t, c):
@@ -104,18 +122,38 @@
         def _():
             pltpu.make_async_copy(src, dst, recv).start()
 
+    def cross_t(t, c):
+        place = theirs + around(t)
+        pltpu.make_async_remote_copy(
+            blk.at[place], tfl.at[place], tfs_sem, tfr_sem.at[place - theirs],
+            device_id=(flip, q), device_id_type=MESH,
+        ).start()
+        return c
+
+    def around(t):
+        return (z + ((t + 1) // 2) * (2 * (t % 2) - 1) + 8) % 8
+
     def send_t(t, c):
-        zi = t // 2
-        dz = ((zi + 1) // 2) * (2 * (zi % 2) - 1)
-        k = ((ylo + t % 2) % 2) * 8 + (z + dz + 8) % 8
+        k = ours + around(t)
         send_block(blk.at[k], tsl.at[pl.ds(2 * p, 2)], ts_sem, tr_sem, k)
         return c
 
-    lax.fori_loop(0, NI, send_t, 0)
+    def pass_t(t, c):
+        zk = around(t)
+        pltpu.make_async_copy(blk.at[0], tfl.at[ours + zk], tfr_sem.at[zk]).wait()
+        send_block(tfl.at[ours + zk], tsl.at[pl.ds(2 * flip, 2)], ts_sem, tr_sem, ours + zk)
+        return c
+
+    lax.fori_loop(0, 8, cross_t, 0)
+    lax.fori_loop(0, 8, send_t, 0)
+    lax.fori_loop(0, 8, pass_t, 0)
 
     most = vg.at[:, pl.ds(0, 15), 0]
     pltpu.make_async_copy(most, most, vr_sem).wait()
-    other = 2 * r + 1 - core
+    pltpu.make_async_remote_copy(
+        blk.at[pl.ds(ours, 8)], tfl.at[pl.ds(ours, 8)], tgs_sem, tgr_sem,
+        device_id=(flip, q), device_id_type=MESH,
+    ).start()
     swap = pltpu.make_async_remote_copy(
         vg.at[:, :, core], vg.at[:, :, core], xs_sem, xr_sem,
         device_id=(p, other), device_id_type=MESH,
@@ -124,59 +162,79 @@
     swap.wait_send()
     pltpu.make_async_copy(vg.at[:, :, 0], vg.at[:, :, 0], xr_sem).wait()
 
-    def ladder(source, store):
-        def first(s, c):
-            for h in range(2):
-                piece = source[s, h * 256:(h + 1) * 256, :]
-                for l in range(3):
-                    inner[s, l, h * 256:(h + 1) * 256, :] = lax.dot_general(
-                        piece, vg[l].reshape(512, 512), (((1,), (1,)), ((), ())),
-                        preferred_element_type=jnp.float32,
-                    ).astype(jnp.bfloat16)
+    def inner_half(s, c):
+        for h in range(2):
+            piece = tb[s, h * 256:(h + 1) * 256, :]
+            for l in range(3):
+                inner[s, l, h * 256:(h + 1) * 256, :] = lax.dot_general(
+                    piece, vg[l].reshape(512, 512), (((1,), (1,)), ((), ())),
+                    preferred_element_type=jnp.float32,
+                ).astype(jnp.bfloat16)
+        return c
+
+    def outer(s, first, last, left, right):
+        total = None
+        for l in range(3):
+            term = jnp.dot(
+                vg[l, first * 4:last * 4].reshape((last - first) * B, 512),
+                inner[s, l, :, left * B:right * B], preferred_element_type=jnp.float32,
+            )
+            total = term if total is None else total + term
+        return total
+
+    def ladder_blocks(turn):
+        lax.fori_loop(0, 2, inner_half, 0)
+        for plane, parts in enumerate((((0, 1, 0, 4), (1, 3, 2, 4)), ((3, 4, 0, 4), (1, 3, 0, 2)))):
+            def one_pair(s, c, parts=parts, plane=plane):
+                for first, last, left, right in parts:
+                    total = outer(s, first, last, left, right)
+                    for ka in range(first, last):
+                        for kb in range(left, right):
+                            zk = PLACES.index((ka, kb)) - 8 * plane
+                            lblk[turn, zk, s] = total[
+                                (ka - first) * B:(ka - first + 1) * B, (kb - left) * B:(kb - left + 1) * B
+                            ].astype(jnp.bfloat16)
+                return c
+
+            @pl.when(ylo == plane)
+            def _():
+                lax.fori_loop(0, 2, one_pair, 0)
+
+        origin = (p, flip)[turn]
+
+        def send_l(t, c):
+            zk = (z + 3 * NI - r - t) % 8
+            send_block(
+                lblk.at[turn, zk], lsl.at[pl.ds(2 * origin, 2)], ls_sem, lr_sem.at[origin], ours + zk
+            )
             return c
 
-        def second(s, c):
-            for h in range(2):
-                total = None
-                for l in range(3):
-                    term = jnp.dot(
-                        vg[l, h * 8:(h + 1) * 8].reshape(256, 512), inner[s, l],
-                        preferred_element_type=jnp.float32,
-                    )
-                    total = term if total is None else total + term
-                store(s, h, total)
-            return c
-
-        lax.fori_loop(0, 2, first, 0)
-        lax.fori_loop(0, 2, second, 0)
-
-    def store_blocks(s, h, total):
-        for place, (ka, kb) in enumerate(PLACES):
-            if ka // 2 == h:
-                lblk[place, s] = total[(ka % 2) * B:(ka % 2 + 1) * B, kb * B:(kb + 1) * B].astype(jnp.bfloat16)
-
-    ladder(tb, store_blocks)
-
-    def send_l(t, c):
-        k = (p + 2 * NI - r - t) % NI
-        send_block(lblk.at[k], lsl.at[pl.ds(2 * p, 2)], ls_sem, lr_sem.at[p], k)
-        return c
-
-    lax.fori_loop(0, NI, send_l, 0)
+        lax.fori_loop(0, 8, send_l, 0)
+
+    ladder_blocks(0)
 
     def mixing(source):
         def group(g, c):
-            lines = pl.ds(pl.multiple_of(g * 16, 16), 16)
+            lines = [pl.ds(pl.multiple_of(g * 32 + 16 * h, 16), 16) for h in range(2)]
+            pieces = [source[:, at, :].reshape(512, B) for at in lines]
             got = jnp.dot(
-                kron[...], source[:, lines, :].reshape(512, B), preferred_element_type=jnp.float32
+                kron[...], jnp.concatenate(pieces, axis=1), preferred_element_type=jnp.float32
             )
-            mix[:, lines, :] = got.reshape(NJ, 16, B)
+            for h in range(2):
+                mix[:, lines[h], :] = got[:, h * B:(h + 1) * B].reshape(NJ, 16, B)
             return c
 
-        lax.fori_loop(0, B // 16, group, 0)
+        lax.fori_loop(0, B // 32, group, 0)
 
     pltpu.make_async_copy(tsl, tsl, tr_sem).wait()
     mixing(tsl)
+
+    half_places = pl.ds(0, 8)
+    pltpu.make_async_copy(blk.at[half_places], blk.at[half_places], tgr_sem).wait()
+    for s in range(2):
+        for place, (ka, kb) in enumerate(PLACES):
+            tb[s, ka * B:(ka + 1) * B, kb * B:(kb + 1) * B] = tfl[place, s]
+    ladder_blocks(1)
 
     def send_mirror(src, dst, send, recv, i):
         alone = (mirror == p) & (i == q)
@@ -192,12 +250,14 @@
             pltpu.make_async_copy(src, dst, recv).start()
 
     def halves(t, c):
-        k = (p + r + t) % NI
-        pltpu.make_async_copy(lblk.at[0], lsl.at[pl.ds(2 * k, 2)], lr_sem.at[k]).wait()
+        k = ((ylo + t // 8) % 2) * 8 + (z + r + t) % 8
+        pltpu.make_async_copy(lblk.at[0, 0], lsl.at[pl.ds(2 * k, 2)], lr_sem.at[k]).wait()
         for s in range(2):
             i = 2 * k + s
-            hs[i] = (mix[i] + lsl[i].astype(jnp.float32)).astype(jnp.bfloat16)
-            send_mirror(hs.at[i], hm.at[q], hs_sem, hr_sem.at[q], i)
+            half = (mix[i] + lsl[i].astype(jnp.float32)).astype(jnp.bfloat16).astype(jnp.float32)
+            hst[i] = jnp.transpose(half).astype(jnp.bfloat16)
+            send_mirror(hst.at[i], hm.at[q], hs_sem, hr_sem.at[q], i)
+            hs[i] = half.astype(jnp.bfloat16)
         return c
 
     lax.fori_loop(0, NI, halves, 0)
@@ -212,11 +272,11 @@
     occ_j = occ_ref[q]
 
     def updates(t, c):
-        k = (r + 2 * NI - mirror - t) % NI
+        k = ((r // 8 + t) % 2) * 8 + (r + 2 * NI - z - t // 2) % 8
         for s in range(2):
             i = 2 * k + s
             pltpu.make_async_copy(hs.at[0], hm.at[i], hr_sem.at[i]).wait()
-            residual = hs[i].astype(jnp.float32) + jnp.transpose(hm[i].astype(jnp.float32))
+            residual = hs[i].astype(jnp.float32) + hm[i].astype(jnp.float32)
             denominator = ((occ_ref[i] + occ_j) - va_block) - vb
             us[i] = (residual / denominator).astype(jnp.bfloat16)
         send_block(us.at[pl.ds(2 * k, 2)], uh.at[p], us_sem, ur_sem, k)
@@ -230,7 +290,7 @@
         k = (r + t) % NI
         for s in range(2):
             i = 2 * k + s
-            ms[i] = mix[i].astype(jnp.bfloat16)
+            ms[i] = jnp.transpose(mix[i]).astype(jnp.bfloat16)
             send_mirror(ms.at[i], hm2.at[q], ms_sem, mr_sem.at[q], i)
         return c
 
@@ -241,7 +301,7 @@
         for s in range(2):
             i = 2 * k + s
             pltpu.make_async_copy(ms.at[0], hm2.at[i], mr_sem.at[i]).wait()
-            ws[i] = (mix[i] + jnp.transpose(hm2[i].astype(jnp.float32))).astype(jnp.bfloat16)
+            ws[i] = (mix[i] + hm2[i].astype(jnp.float32)).astype(jnp.bfloat16)
         send_block(ws.at[pl.ds(2 * k, 2)], wh.at[p], ws_sem, wr_sem, k)
         return c
 
@@ -252,10 +312,14 @@
         for place, (ka, kb) in enumerate(PLACES):
             tb[s, ka * B:(ka + 1) * B, kb * B:(kb + 1) * B] = uh[place, s]
 
-    def store_plain(s, h, total):
-        lu[s, h * 256:(h + 1) * 256, :] = total
-
-    ladder(tb, store_plain)
+    lax.fori_loop(0, 2, inner_half, 0)
+
+    def outer_half(s, c):
+        for h in range(2):
+            lu[s, h * 256:(h + 1) * 256, :] = outer(s, 2 * h, 2 * h + 2, 0, 4)
+        return c
+
+    lax.fori_loop(0, 2, outer_half, 0)
 
     pltpu.make_async_copy(wh, wh, wr_sem).wait()
     for ka in range(4):
@@ -272,8 +336,10 @@
 
     pltpu.make_async_copy(most, most, vs_sem).wait()
     rest = pl.ds(0, NI - 1)
-    pltpu.make_async_copy(blk.at[rest], blk.at[rest], ts_sem).wait()
-    pltpu.make_async_copy(lblk.at[rest], lblk.at[rest], ls_sem).wait()
+    pltpu.make_async_copy(lsl.at[pl.ds(0, 28)], lsl.at[pl.ds(0, 28)], ts_sem).wait()
+    pltpu.make_async_copy(lsl.at[pl.ds(0, 28)], lsl.at[pl.ds(0, 28)], ls_sem).wait()
+    pltpu.make_async_copy(blk.at[half_places], blk.at[half_places], tfs_sem).wait()
+    pltpu.make_async_copy(blk.at[half_places], blk.at[half_places], tgs_sem).wait()
     pltpu.make_async_copy(uh.at[rest], uh.at[rest], us_sem).wait()
     pltpu.make_async_copy(wh.at[rest], wh.at[rest], ws_sem).wait()
     alone = mirror == p
@@ -296,7 +362,7 @@
     vmem = pl.BlockSpec(memory_space=pltpu.VMEM)
     out = pl.pallas_call(
         kernel,
-        out_shape=jax.ShapeDtypeStruct((2, 512, 512), f32),
+        out_shape=pltpu.VMEM((2, 512, 512), f32),
         in_specs=[
             pl.BlockSpec(memory_space=pl.ANY), vmem, vmem,
             pl.BlockSpec(memory_space=pltpu.SMEM), vmem,
@@ -305,14 +371,16 @@
         scratch_shapes=[
             pltpu.VMEM((2, 512, 512), f32),
             pltpu.VMEM((2, 512, 512), bf),
+            pltpu.VMEM((NI, 2, B, B), bf),
             pltpu.VMEM((3, 16, 2, 16, 512), bf),
             pltpu.VMEM((512, 512), bf),
             pltpu.VMEM((2, 3, 512, 512), bf),
             pltpu.VMEM((NI, 2, B, B), bf),
             pltpu.VMEM((NJ, B, B), bf),
-            pltpu.VMEM((NI, 2, B, B), bf),
+            pltpu.VMEM((2, 8, 2, B, B), bf),
             pltpu.VMEM((NJ, B, B), bf),
             pltpu.VMEM((NJ, B, B), f32),
+            pltpu.VMEM((NJ, B, B), bf),
             pltpu.VMEM((NJ, B, B), bf),
             pltpu.VMEM((NJ, B, B), bf),
             pltpu.VMEM((NJ, B, B), bf),
@@ -323,6 +391,7 @@
             pltpu.VMEM((NI, 2, B, B), bf),
             pltpu.VMEM((2, 512, 512), f32),
             dma, dma, dma, dma, dma, dma, dma,
+            dma, dma((8,)), dma, dma,
             dma, dma((NI,)), dma, dma((NJ,)),
             dma, dma, dma, dma((NJ,)), dma, dma,
         ],

time: 160 us -> 151 us (0.944)
  the two profiles are of different devices: /device:TPU:29 before, /device:TPU:31 now
where the time goes in v2:
time: 151 us
  Pallas kernels  149 us (99%)
    pallas_call x1, Pallas kernels, local(): pl.pallas_call(kernel, out_shape=pltpu.VMEM((2, 512, 512), f32), in_specs...  149 us

profile of v2, /device:TPU:31, one launch (start us, length us, event | category | flops | bytes accessed | tf_op | source)
XLA Modules:
  0.0 150.8 jit_solution(10909547423802099515)
XLA Ops:
  0.0 149.5 %doubles.1 = f32[2,512,512]{2,1,0:T(8,128)S(1)} custom-call(f32[2,512,512]{2,1,0:T(8,128)} %bitcast.6, bf16[3,16,512]{2,1,0:T(8,128)(2,1)} %vec_ref.1, bf16[32,32]{1,0:T(8,128)(2,1)} %fock_ref.1, f32[32]{0:T(128)} %occ_ref.1, f32[4,128]{1,0:T(4,128)} %bitcast.7), custom_call_target="tpu_custom_call" | custom-call | tf_op jit(solution)/shard_map/doubles/pallas_call | solution.py:363
  149.5 1.3 copy.8

commit v3 on v2

--- a/solution.py
+++ b/solution.py
@@ -108,9 +108,6 @@
         send_vec(0, t)
         return c
 
-    lax.fori_loop(0, 12, send_vec_far, 0)
-    lax.fori_loop(1, 4, send_vec_near, 0)
-
     def send_block(src, dst, send, recv, k):
         @pl.when(k != p)
         def _():
@@ -146,14 +143,16 @@
 
     lax.fori_loop(0, 8, cross_t, 0)
     lax.fori_loop(0, 8, send_t, 0)
+    lax.fori_loop(0, 12, send_vec_far, 0)
+    lax.fori_loop(1, 4, send_vec_near, 0)
     lax.fori_loop(0, 8, pass_t, 0)
-
-    most = vg.at[:, pl.ds(0, 15), 0]
-    pltpu.make_async_copy(most, most, vr_sem).wait()
     pltpu.make_async_remote_copy(
         blk.at[pl.ds(ours, 8)], tfl.at[pl.ds(ours, 8)], tgs_sem, tgr_sem,
         device_id=(flip, q), device_id_type=MESH,
     ).start()
+
+    most = vg.at[:, pl.ds(0, 15), 0]
+    pltpu.make_async_copy(most, most, vr_sem).wait()
     swap = pltpu.make_async_remote_copy(
         vg.at[:, :, core], vg.at[:, :, core], xs_sem, xr_sem,
         device_id=(p, other), device_id_type=MESH,
@@ -161,6 +160,9 @@
     swap.start()
     swap.wait_send()
     pltpu.make_async_copy(vg.at[:, :, 0], vg.at[:, :, 0], xr_sem).wait()
+
+    def turn_of(t):
+        return t // 2 + 4 * (t % 2)
 
     def inner_half(s, c):
         for h in range(2):
@@ -203,7 +205,7 @@
         origin = (p, flip)[turn]
 
         def send_l(t, c):
-            zk = (z + 3 * NI - r - t) % 8
+            zk = (z + 3 * NI - r - turn_of(t)) % 8
             send_block(
                 lblk.at[turn, zk], lsl.at[pl.ds(2 * origin, 2)], ls_sem, lr_sem.at[origin], ours + zk
             )
@@ -250,7 +252,7 @@
             pltpu.make_async_copy(src, dst, recv).start()
 
     def halves(t, c):
-        k = ((ylo + t // 8) % 2) * 8 + (z + r + t) % 8
+        k = ((ylo + t // 8) % 2) * 8 + (z + r + turn_of(t % 8)) % 8
         pltpu.make_async_copy(lblk.at[0, 0], lsl.at[pl.ds(2 * k, 2)], lr_sem.at[k]).wait()
         for s in range(2):
             i = 2 * k + s
@@ -272,7 +274,7 @@
     occ_j = occ_ref[q]
 
     def updates(t, c):
-        k = ((r // 8 + t) % 2) * 8 + (r + 2 * NI - z - t // 2) % 8
+        k = ((r // 8 + t) % 2) * 8 + (r + 2 * NI - z - turn_of(t // 2)) % 8
         for s in range(2):
             i = 2 * k + s
             pltpu.make_async_copy(hs.at[0], hm.at[i], hr_sem.at[i]).wait()
@@ -287,7 +289,7 @@
     mixing(us)
 
     def send_mix(t, c):
-        k = (r + t) % NI
+        k = ((yhi + z // 4 + 2 * (mirror // 8) + t) % 4) * 4 + (x + z + t // 4) % 4
         for s in range(2):
             i = 2 * k + s
             ms[i] = jnp.transpose(mix[i]).astype(jnp.bfloat16)
@@ -297,7 +299,7 @@
     lax.fori_loop(0, NI, send_mix, 0)
 
     def sums(t, c):
-        k = (r + NI - t) % NI
+        k = ((yhi + 24 - z // 4 - 2 * ylo - t) % 4) * 4 + (x + 16 - z - t // 4) % 4
         for s in range(2):
             i = 2 * k + s
             pltpu.make_async_copy(ms.at[0], hm2.at[i], mr_sem.at[i]).wait()

time: 151 us -> 140 us (0.927)
  the two profiles are of different devices: /device:TPU:31 before, /device:TPU:1 now
where the time goes in v3:
time: 140 us; the launch traced here: 139 us
  Pallas kernels  138 us (99%)
    pallas_call x1, Pallas kernels, local(): pl.pallas_call(kernel, out_shape=pltpu.VMEM((2, 512, 512), f32), in_specs...  138 us

profile of v3, /device:TPU:1, one launch (start us, length us, event | category | flops | bytes accessed | tf_op | source)
XLA Modules:
  0.0 139.5 jit_solution(6235081428740258844)
XLA Ops:
  0.0 138.2 %doubles.1 = f32[2,512,512]{2,1,0:T(8,128)S(1)} custom-call(f32[2,512,512]{2,1,0:T(8,128)} %bitcast.6, bf16[3,16,512]{2,1,0:T(8,128)(2,1)} %vec_ref.1, bf16[32,32]{1,0:T(8,128)(2,1)} %fock_ref.1, f32[32]{0:T(128)} %occ_ref.1, f32[4,128]{1,0:T(4,128)} %bitcast.7), custom_call_target="tpu_custom_call" | custom-call | tf_op jit(solution)/shard_map/doubles/pallas_call | solution.py:365
  138.2 1.3 copy.8

commit v4 on v3

--- a/solution.py
+++ b/solution.py
@@ -323,18 +323,24 @@
 
     lax.fori_loop(0, 2, outer_half, 0)
 
-    pltpu.make_async_copy(wh, wh, wr_sem).wait()
     for ka in range(4):
         va_block = jnp.transpose(jnp.broadcast_to(vir_ref[ka:ka + 1, :], (B, B)))
         for kb in range(4):
             place = PLACES.index((ka, kb))
             at = (slice(ka * B, (ka + 1) * B), slice(kb * B, (kb + 1) * B))
             for s in range(2):
-                denominator = ((occ_ref[2 * p + s] + occ_j) - va_block) - vir_ref[kb:kb + 1, :]
-                residual = 2.0 * lu[(s,) + at] + wh[place, s].astype(jnp.float32)
-                out_ref[(s,) + at] = (
-                    t0[(s,) + at] + 2.0 * uh[place, s].astype(jnp.float32) + residual / denominator
+                inverse = 1.0 / (((occ_ref[2 * p + s] + occ_j) - va_block) - vir_ref[kb:kb + 1, :])
+                lu[(s,) + at] = (
+                    t0[(s,) + at] + 2.0 * uh[place, s].astype(jnp.float32)
+                    + 2.0 * lu[(s,) + at] * inverse
                 )
+                t0[(s,) + at] = inverse
+
+    pltpu.make_async_copy(wh, wh, wr_sem).wait()
+    for place, (ka, kb) in enumerate(PLACES):
+        at = (slice(ka * B, (ka + 1) * B), slice(kb * B, (kb + 1) * B))
+        for s in range(2):
+            out_ref[(s,) + at] = lu[(s,) + at] + wh[place, s].astype(jnp.float32) * t0[(s,) + at]
 
     pltpu.make_async_copy(most, most, vs_sem).wait()
     rest = pl.ds(0, NI - 1)

time: 140 us -> 139 us (level)
  no operation moved by 1% of the time
where the time goes in v4:
time: 139 us
  Pallas kernels  138 us (99%)
    pallas_call x1, Pallas kernels, local(): pl.pallas_call(kernel, out_shape=pltpu.VMEM((2, 512, 512), f32), in_specs...  138 us

profile of v4, /device:TPU:1, one launch (start us, length us, event | category | flops | bytes accessed | tf_op | source)
XLA Modules:
  0.0 139.1 jit_solution(14182866752032940693)
XLA Ops:
  0.0 137.8 %doubles.1 = f32[2,512,512]{2,1,0:T(8,128)S(1)} custom-call(f32[2,512,512]{2,1,0:T(8,128)} %bitcast.6, bf16[3,16,512]{2,1,0:T(8,128)(2,1)} %vec_ref.1, bf16[32,32]{1,0:T(8,128)(2,1)} %fock_ref.1, f32[32]{0:T(128)} %occ_ref.1, f32[4,128]{1,0:T(4,128)} %bitcast.7), custom_call_target="tpu_custom_call" | custom-call | tf_op jit(solution)/shard_map/doubles/pallas_call | solution.py:371
  137.8 1.3 copy.8
